TPU v7x, 512 devices: a whole 4x4x16 slice. The times are simulated.
512 devices in a mesh: vocab: 64 (over z, x_lo, core), hid: 8 (over x_hi, y).
Axes of the slice: x: 4 (x_hi: 2, x_lo: 2; x = x_hi * 2 + x_lo), y: 4, z: 16, core: 2. Of those that a mesh axis runs over, the one named last changes fastest.
Arguments:
- posterior: bfloat16 [512, 16384], P(None, 'vocab'), may hold values from 1.9e-09 to 1, as said below
- transition: bfloat16 [16384, 16384], P('vocab', 'hid'), may hold values from 1e-07 to 1, as said below
- emission: bfloat16 [16384, 16384], P('hid', 'vocab'), may hold values from 6e-06 to 90, as said below
- advance: bfloat16 [256, 16384], P(None, 'hid'), may hold values from 0.0099487305 to 1
- dfa_state: int32 [512], replicated, may hold values from 0 to 255
- edge_next: int32 [256, 8], replicated, may hold values from 0 to 255
- token_edge: int32 [256, 16384], P(None, 'vocab'), may hold values from 0 to 7
- allowed: int32 [512, 128], P(None, 'vocab'), may hold values from 0 to 1, as said below
Outputs:
- constrained_logprob: float32 [512, 16384], P('hid', 'vocab')
Inputs may be any that keep to these rules, and one draw needn't show every extreme that they name: `allowed`: every request allows at least one block. `posterior`: positive. `transition`: positive. `emission`: positive.
All inputs are finite; a program needn't handle non-finite values.
Results may differ from a plain program's by a relative error of at most 0.0015.
Values may be sent and summed in bfloat16 or wider, within the bound.
A program may use at most 64 MiB of HBM per device.

v0:
```python
import jax
import jax.numpy as jnp
from jax import lax
from jax.sharding import PartitionSpec as P

BLK = 128


def request_scores(prior_rows, dfa_state, edge_next, token_edge, allowed, advance, emission):
    row_count = prior_rows.shape[0]
    successor = jnp.take(edge_next, dfa_state, axis=0)
    look_rows = jnp.take(advance, successor, axis=0)
    weighted = (prior_rows.astype(jnp.float32)[:, None, :] * look_rows.astype(jnp.float32)).astype(
        jnp.bfloat16
    )
    slot_count = successor.shape[1]
    flattened = weighted.reshape(row_count * slot_count, weighted.shape[2])
    candidate = jnp.dot(flattened, emission, preferred_element_type=jnp.float32).reshape(
        row_count, slot_count, emission.shape[1]
    )
    edge_slots = jnp.take(token_edge, dfa_state, axis=0)
    labels = jnp.arange(slot_count, dtype=jnp.int32)
    chosen = jnp.sum(
        jnp.where(edge_slots[:, None, :] == labels[None, :, None], candidate, jnp.float32(0.0)),
        axis=1,
    )
    token_mask = jnp.repeat(allowed, BLK, axis=1)
    return jnp.where(token_mask > 0, chosen, jnp.float32(0.0))


def body(posterior, transition, emission, advance, dfa_state, edge_next, token_edge, allowed):
    prior_own = lax.psum_scatter(
        jnp.dot(posterior, transition, preferred_element_type=jnp.float32),
        "vocab",
        scatter_dimension=0,
        tiled=True,
    ).astype(jnp.bfloat16)
    partials = request_scores(
        lax.all_gather(prior_own, "vocab", axis=0, tiled=True),
        dfa_state,
        edge_next,
        token_edge,
        allowed,
        advance,
        emission,
    )
    scores = lax.psum_scatter(
        partials.astype(jnp.bfloat16), "hid", scatter_dimension=0, tiled=True
    ).astype(jnp.float32)
    local_rows = scores.shape[0]
    first_local = lax.axis_index("hid") * local_rows
    totals = lax.psum(jnp.sum(scores, axis=1), "vocab")
    mask_rows = lax.dynamic_slice_in_dim(allowed, first_local, local_rows, 0)
    token_mask = jnp.repeat(mask_rows, BLK, axis=1) > 0
    safe = jnp.where(token_mask, scores, jnp.float32(1.0))
    return jnp.where(token_mask, jnp.log(safe) - jnp.log(totals)[:, None], jnp.float32(0.0))


def solution(mesh):
    in_specs = (
        P(None, "vocab"),
        P("vocab", "hid"),
        P("hid", "vocab"),
        P(None, "hid"),
        P(),
        P(),
        P(None, "vocab"),
        P(None, "vocab"),
    )
    out_specs = P("hid", "vocab")
    return jax.shard_map(body, mesh=mesh, in_specs=in_specs, out_specs=out_specs, check_vma=False)
```

profile of v0, /device:TPU:4, one launch (start us, length us, event | category | flops | bytes accessed | tf_op | source)
XLA Modules:
  0.0 602.1 jit_solution(13615866778587981965)
XLA Ops:
  6.5 0.0 copy-start
  6.5 0.0 copy-start.1
  6.5 0.0 reduce-scatter.3.cloned.1.call-start
  6.5 4.0 fusion.9
  10.6 0.0 reduce-scatter.3.cloned.1.call-update
  10.6 0.0 all-gather.2.cloned.1.call-start
  10.7 236.6 %reduce-scatter.3.cloned.1.call-done = f32[8,2048]{1,0:T(8,128)} async-done(((f32[512,2048]{1,0:T(8,128)}), f32[8,2048]{1,0:T(8,128)}) %reduce-scatter.3.cloned.1.call-update) | async-done | bytes 65552 | tf_op jit(solution)/shard_map/reduce_scatter | solution.py:32
  247.2 1.5 convert_element_type.22
  248.7 0.0 all-gather.2.cloned.1.call-update
  248.7 0.0 reduce-scatter.5.cloned.1.call-start
  248.8 0.7 broadcast_compare_fusion
  249.5 0.3 copy.18
  249.8 0.8 copy.15
  250.6 0.7 compare_select_fusion.2
  251.3 1.0 gather_fusion.1
  252.3 0.7 compare_and_fusion.1
  253.0 0.2 compare_and_fusion
  253.2 0.1 copy.16
  253.3 0.1 compare_select_fusion
  253.4 0.1 reshape.104
  253.6 0.0 copy-done.1
  253.6 1.6 gather_fusion
  255.2 0.0 copy-done
  255.2 0.0 copy-start.2
  255.2 21.0 %gather_fusion.2 = bf16[4096,2048]{1,0:T(8,128)(2,1)} fusion(bf16[256,2048]{1,0:T(8,128)(2,1)S(1)} %copy-done, s32[4096]{0:T(1024)S(1)} %broadcast_clamp_fusion), kind=kCustom, calls=%fused_computation.2 | custom fusion | bytes 33570816 | tf_op jit(solution)/shard_map/jit(_take)/gather | solution.py:12
  276.2 0.1 broadcast_select_fusion
  276.3 91.9 %all-gather.2.cloned.1.call-done = bf16[512,2048]{1,0:T(8,128)(2,1)} async-done(((bf16[8,2048]{1,0:T(8,128)(2,1)}), bf16[512,2048]{1,0:T(8,128)(2,1)}) %all-gather.2.cloned.1.call-update) | async-done | bytes 2097168 | tf_op jit(solution)/shard_map/all_gather | solution.py:39
  368.2 2.1 convert_element_type.23
  370.3 0.0 copy-done.2
  370.3 33.8 %select_reduce_fusion = bf16[512,256]{1,0:T(8,128)(2,1)S(1)} fusion(s32[512,256]{1,0:T(8,128)S(1)} %broadcast_select_fusion, bf16[512,8,2048]{2,1,0:T(8,128)(2,1)} %bitcast.16, f32[512,2048]{1,0:T(8,128)S(1)} %convert_element_type.23, pred[512,8]{0,1:T(8,128)(4,1)S(1)} %copy.16, bf16[2048,256]{1,0:T(8,128)(2,1)S(1)} %copy-done.2), kind=kOutput, calls=%fused_computation.9 | convolution fusion | flops 4331536384 | bytes 22810624 | tf_op jit(solution)/shard_map/dot_general | solution.py:18
  404.2 0.8 select_convert_fusion
  404.9 0.0 reduce-scatter.5.cloned.1.call-update
  405.0 0.8 dynamic-slice_compare_fusion
  405.7 0.1 copy.14
  405.8 80.3 %reduce-scatter.5.cloned.1.call-done = bf16[64,256]{1,0:T(8,128)(2,1)} async-done(((bf16[512,256]{1,0:T(8,128)(2,1)}), bf16[64,256]{1,0:T(8,128)(2,1)}) %reduce-scatter.5.cloned.1.call-update) | async-done | bytes 32784 | tf_op jit(solution)/shard_map/reduce_scatter | solution.py:47
  486.2 0.9 convert_reduce_fusion
  487.0 106.9 %psum.7 = f32[64]{0:T(128)S(1)} all-reduce(f32[64]{0:T(128)S(1)} %convert_reduce_fusion), channel_id=1, replica_groups=mesh['vocab'=64,'hid'=8] {'vocab'}, use_global_device_ids=true, to_apply=%region_4.5 | all-reduce | flops 64 | bytes 512 | tf_op jit(solution)/shard_map/psum | solution.py:52
  593.9 0.1 broadcast_in_dim.61
  594.1 1.5 fusion.7
  (4 shorter events, 0.1 us)
Async XLA Ops:
  6.5 248.7 %copy-start = (bf16[256,2048]{1,0:T(8,128)(2,1)S(1)}, bf16[256,2048]{1,0:T(8,128)(2,1)}, u32[]{:S(2)}) copy-start(bf16[256,2048]{1,0:T(8,128)(2,1)} %param.11) | copy-start | bytes 3145732
  6.5 247.1 %copy-start.1 = (s32[256,256]{1,0:T(8,128)S(1)}, s32[256,256]{1,0:T(8,128)}, u32[]{:S(2)}) copy-start(s32[256,256]{1,0:T(8,128)} %param.14) | copy-start | bytes 786436
  6.5 240.7 %reduce-scatter.3.cloned.1.call-start = ((), (), s32[]{:S(2)}) async-start(), calls=%async_computation.2 | async-start | bytes 4259840 | tf_op jit(solution)/shard_map/reduce_scatter | solution.py:32
  10.6 357.6 %all-gather.2.cloned.1.call-start = ((), (), s32[]{:S(2)}) async-start(), calls=%async_computation.3 | async-start | bytes 2129920 | tf_op jit(solution)/shard_map/all_gather | solution.py:39
  248.7 237.5 %reduce-scatter.5.cloned.1.call-start = ((), (), s32[]{:S(2)}) async-start(), calls=%async_computation.4 | async-start | bytes 294912 | tf_op jit(solution)/shard_map/reduce_scatter | solution.py:47
  255.2 115.1 %copy-start.2 = (bf16[2048,256]{1,0:T(8,128)(2,1)S(1)}, bf16[2048,256]{1,0:T(8,128)(2,1)}, u32[]{:S(2)}) copy-start(bf16[2048,256]{1,0:T(8,128)(2,1)} %param.10) | copy-start | bytes 3145732
Sparse Core Ops, SparseCore 0:
  10.7 236.4 reduce-scatter.2
  249.6 118.5 all-gather.1
  405.1 81.0 reduce-scatter.4
where the time goes:
time: 603 us; the launch traced here: 602 us
  waiting for transfers between devices  409 us (68%)
  blocking collectives  107 us (18%)
  matrix products  37.9 us (6%)
  local copies, waits for them, and re-layouts  25.2 us (4%)
  between operations  13.2 us (2%)
  other arithmetic  9.95 us (2%)
    reduce_scatter x1, waiting for transfers between devices, body(): lax.psum_scatter(jnp.dot(posterior, transition, preferred_element_type=jn...  237 us
    psum x1, blocking collectives, body(): totals = lax.psum(jnp.sum(scores, axis=1), 'vocab')  107 us
    all_gather x1, waiting for transfers between devices, body(): lax.all_gather(prior_own, 'vocab', axis=0, tiled=True)  91.9 us
    reduce_scatter x1, waiting for transfers between devices, body(): lax.psum_scatter(partials.astype(jnp.bfloat16), 'hid', scatter_dimension=...  80.3 us
    dot_general x1, matrix products, request_scores(): jnp.dot(flattened, emission, preferred_element_type=jnp.float32)  33.8 us
    gather x1, local copies, waits for them, and re-layouts, request_scores(): look_rows = jnp.take(advance, successor, axis=0)  21 us
  transfers between devices with their start and end apart: 3, of which 3 were waited for; matrix products, arithmetic and copies ran while one was open for 5% of the time, Pallas kernels for 0%

commit v1 on v0

--- a/solution.py
+++ b/solution.py
@@ -49,7 +49,7 @@
     ).astype(jnp.float32)
     local_rows = scores.shape[0]
     first_local = lax.axis_index("hid") * local_rows
-    totals = lax.psum(jnp.sum(scores, axis=1), "vocab")
+    totals = jnp.sum(lax.all_gather(jnp.sum(scores, axis=1), "vocab"), axis=0)
     mask_rows = lax.dynamic_slice_in_dim(allowed, first_local, local_rows, 0)
     token_mask = jnp.repeat(mask_rows, BLK, axis=1) > 0
     safe = jnp.where(token_mask, scores, jnp.float32(1.0))

time: 603 us -> 706 us (1.17)
  blocking collectives: 107 us -> 210 us
    unnamed x0 -> x1, blocking collectives: none -> 210 us
    psum x1 -> x0, blocking collectives: 107 us -> none  [body(): totals = lax.psum(jnp.sum(scores, axis=1), 'vocab')]
  transfers between devices with their start and end apart: 3 -> 3, of which waited for: 3 -> 3; matrix products, arithmetic and copies ran while one was open for 5% -> 4% of each run, Pallas kernels for 0% -> 0%
where the time goes in v1:
time: 706 us; the launch traced here: 705 us
  waiting for transfers between devices  407 us (58%)
  blocking collectives  210 us (30%)
  matrix products  37.9 us (5%)
  local copies, waits for them, and re-layouts  26.8 us (4%)
  between operations  13.9 us (2%)
  other arithmetic  9.98 us (1%)
    reduce_scatter x1, waiting for transfers between devices, body(): lax.psum_scatter(jnp.dot(posterior, transition, preferred_element_type=jn...  237 us
    unnamed x1, blocking collectives  210 us
    all_gather x1, waiting for transfers between devices, body(): lax.all_gather(prior_own, 'vocab', axis=0, tiled=True)  91.9 us
    reduce_scatter x1, waiting for transfers between devices, body(): lax.psum_scatter(partials.astype(jnp.bfloat16), 'hid', scatter_dimension=...  78.4 us
    dot_general x1, matrix products, request_scores(): jnp.dot(flattened, emission, preferred_element_type=jnp.float32)  33.8 us
    gather x1, local copies, waits for them, and re-layouts, request_scores(): look_rows = jnp.take(advance, successor, axis=0)  21 us
  transfers between devices with their start and end apart: 3, of which 3 were waited for; matrix products, arithmetic and copies ran while one was open for 4% of the time, Pallas kernels for 0%

profile of v1, /device:TPU:4, one launch (start us, length us, event | category | flops | bytes accessed | tf_op | source)
XLA Modules:
  0.0 705.1 jit_solution(18434296811761582645)
XLA Ops:
  6.5 0.0 copy-start
  6.5 0.0 copy-start.1
  6.5 0.0 reduce-scatter.3.cloned.1.call-start
  6.5 4.0 fusion.9
  10.6 0.0 reduce-scatter.3.cloned.1.call-update
  10.6 0.0 all-gather.3.cloned.1.call-start
  10.7 236.6 %reduce-scatter.3.cloned.1.call-done = f32[8,2048]{1,0:T(8,128)} async-done(((f32[512,2048]{1,0:T(8,128)}), f32[8,2048]{1,0:T(8,128)}) %reduce-scatter.3.cloned.1.call-update) | async-done | bytes 65552 | tf_op jit(solution)/shard_map/reduce_scatter | solution.py:32
  247.2 1.5 convert_element_type.22
  248.7 0.0 all-gather.3.cloned.1.call-update
  248.7 0.0 reduce-scatter.5.cloned.1.call-start
  248.8 0.7 broadcast_compare_fusion
  249.5 0.3 copy.23
  249.8 0.8 copy.20
  250.6 0.7 compare_select_fusion.2
  251.3 1.0 gather_fusion.1
  252.3 0.7 compare_and_fusion.1
  253.0 0.2 compare_and_fusion
  253.2 0.1 copy.21
  253.3 0.1 compare_select_fusion
  253.4 0.1 reshape.106
  253.6 0.0 copy-done.1
  253.6 1.6 gather_fusion
  255.2 0.0 copy-done
  255.2 0.0 copy-start.2
  255.2 21.0 %gather_fusion.2 = bf16[4096,2048]{1,0:T(8,128)(2,1)} fusion(bf16[256,2048]{1,0:T(8,128)(2,1)S(1)} %copy-done, s32[4096]{0:T(1024)S(1)} %broadcast_clamp_fusion), kind=kCustom, calls=%fused_computation.2 | custom fusion | bytes 33570816 | tf_op jit(solution)/shard_map/jit(_take)/gather | solution.py:12
  276.2 0.1 broadcast_select_fusion
  276.3 91.9 %all-gather.3.cloned.1.call-done = bf16[512,2048]{1,0:T(8,128)(2,1)} async-done(((bf16[8,2048]{1,0:T(8,128)(2,1)}), bf16[512,2048]{1,0:T(8,128)(2,1)}) %all-gather.3.cloned.1.call-update) | async-done | bytes 2097168 | tf_op jit(solution)/shard_map/all_gather | solution.py:39
  368.2 2.1 convert_element_type.23
  370.3 0.0 copy-done.2
  370.3 33.8 %select_reduce_fusion = bf16[512,256]{1,0:T(8,128)(2,1)S(1)} fusion(s32[512,256]{1,0:T(8,128)S(1)} %broadcast_select_fusion, bf16[512,8,2048]{2,1,0:T(8,128)(2,1)} %bitcast.17, f32[512,2048]{1,0:T(8,128)S(1)} %convert_element_type.23, pred[512,8]{0,1:T(8,128)(4,1)S(1)} %copy.21, bf16[2048,256]{1,0:T(8,128)(2,1)S(1)} %copy-done.2), kind=kOutput, calls=%fused_computation.9 | convolution fusion | flops 4331536384 | bytes 22810624 | tf_op jit(solution)/shard_map/dot_general | solution.py:18
  404.2 0.8 select_convert_fusion
  404.9 0.0 reduce-scatter.5.cloned.1.call-update
  405.0 0.8 dynamic-slice_compare_fusion
  405.7 0.1 copy.19
  405.8 1.3 dynamic-slice
  407.8 78.4 %reduce-scatter.5.cloned.1.call-done = bf16[64,256]{1,0:T(8,128)(2,1)} async-done(((bf16[512,256]{1,0:T(8,128)(2,1)}), bf16[64,256]{1,0:T(8,128)(2,1)}) %reduce-scatter.5.cloned.1.call-update) | async-done | bytes 32784 | tf_op jit(solution)/shard_map/reduce_scatter | solution.py:47
  486.2 0.9 convert_reduce_fusion
  487.0 0.3 dynamic-update-slice
  487.3 209.6 %all-reduce = f32[4096]{0:T(1024)S(1)} all-reduce(f32[4096]{0:T(1024)S(1)} %dynamic-update-slice), channel_id=2, replica_groups=mesh['vocab'=64,'hid'=8] {'vocab'}, use_global_device_ids=true, to_apply=%add | all-reduce | flops 4096 | bytes 32768
  696.9 0.1 reshape.112
  697.0 0.1 broadcast_in_dim.61
  697.1 1.5 fusion.7
  (6 shorter events, 0.1 us)
Async XLA Ops:
  6.5 248.7 %copy-start = (bf16[256,2048]{1,0:T(8,128)(2,1)S(1)}, bf16[256,2048]{1,0:T(8,128)(2,1)}, u32[]{:S(2)}) copy-start(bf16[256,2048]{1,0:T(8,128)(2,1)} %param.11) | copy-start | bytes 3145732
  6.5 247.1 %copy-start.1 = (s32[256,256]{1,0:T(8,128)S(1)}, s32[256,256]{1,0:T(8,128)}, u32[]{:S(2)}) copy-start(s32[256,256]{1,0:T(8,128)} %param.14) | copy-start | bytes 786436
  6.5 240.7 %reduce-scatter.3.cloned.1.call-start = ((), (), s32[]{:S(2)}) async-start(), calls=%async_computation.2 | async-start | bytes 4259840 | tf_op jit(solution)/shard_map/reduce_scatter | solution.py:32
  10.6 357.6 %all-gather.3.cloned.1.call-start = ((), (), s32[]{:S(2)}) async-start(), calls=%async_computation.3 | async-start | bytes 2129920 | tf_op jit(solution)/shard_map/all_gather | solution.py:39
  248.7 237.5 %reduce-scatter.5.cloned.1.call-start = ((), (), s32[]{:S(2)}) async-start(), calls=%async_computation.4 | async-start | bytes 294912 | tf_op jit(solution)/shard_map/reduce_scatter | solution.py:47
  255.2 115.1 %copy-start.2 = (bf16[2048,256]{1,0:T(8,128)(2,1)S(1)}, bf16[2048,256]{1,0:T(8,128)(2,1)}, u32[]{:S(2)}) copy-start(bf16[2048,256]{1,0:T(8,128)(2,1)} %param.10) | copy-start | bytes 3145732
Sparse Core Ops, SparseCore 0:
  10.7 236.4 reduce-scatter.2
  249.6 118.5 all-gather.2
  405.1 81.0 reduce-scatter.4
